TPU v7x, 32 devices: a whole 2x2x4 slice. The times are simulated.
32 devices in a mesh: col: 8 (over z, y), row: 4 (over x, core).
Axes of the slice: x: 2, y: 2, z: 4, core: 2. Of those that a mesh axis runs over, the one named last changes fastest.
Arguments:
- factor: float32 [8, 512, 1024], P('col', 'row'), may hold values from -0.6 to 0.6
- pattern: int32 [8, 4, 8], replicated, may hold values from 0 to 1, as said below
- order: int32 [8], replicated, may hold values from 0 to 7, each once
- targets: int32 [2, 2], replicated, may hold values from 0 to 3, as said below
- panels: float32 [512, 512], P('row'), may hold values from -6 to 6
Outputs:
- carried: float32 [8, 512, 512], P('col', 'row')
Inputs may be any that keep to these rules, and one draw needn't show every extreme that they name: `pattern`: 0 or 1 for each block of a supernode's rows and factored columns; the share of present blocks differs between supernodes. `targets`: every row block 0..3 is named at least once.
All inputs are finite; a program needn't handle non-finite values.
Results may differ from a plain program's by a relative error of at most 0.0001.
Values sent between devices are 32-bit elements; how exact they have to be, the bound alone decides.
No kernel may reach another device: no remote copies, remote signals or barrier semaphores. Data moves between devices by JAX's collectives and lax.ppermute only.
A program may use at most 128 MiB of HBM per device.

v0:
```python
import jax
import jax.numpy as jnp
from jax import lax
from jax.sharding import PartitionSpec as P

BLOCK = 128


def carried_in(value, axis, combine, identity):
    devices, place = (lax.axis_size(axis), lax.axis_index(axis))
    everything = lax.all_gather(value, axis)
    start = jnp.broadcast_to(jnp.asarray(identity, value.dtype), value.shape)

    def step(k, before):
        reached = k < place
        new = combine(before, everything[k])
        return jnp.where(reached, new, before)

    return lax.fori_loop(0, devices, step, start)


def product(masked, strips):
    return lax.dot_general(
        masked,
        strips,
        (((1,), (1,)), ((), ())),
        precision=lax.Precision.HIGHEST,
        preferred_element_type=jnp.float32,
    )


def combine(earlier, later):
    return earlier + later


def body(factor, pattern, order, targets, panels):
    owner_rows = factor[0]
    local_count = owner_rows.shape[0]
    width = owner_rows.shape[1]
    position = lax.axis_index("col")
    row_place = lax.axis_index("row")
    chain_length = order.shape[0]
    supernode = jnp.sum(jnp.where(jnp.arange(chain_length, dtype=jnp.int32) == position, order, 0))
    picked = (jnp.arange(pattern.shape[0], dtype=jnp.int32) == supernode).astype(jnp.int32)
    owner_pattern = jnp.sum(picked[:, None, None] * pattern, axis=0)
    local_blocks = local_count // BLOCK
    col_blocks = width // BLOCK
    local_pattern = lax.dynamic_slice_in_dim(
        owner_pattern, row_place * local_blocks, local_blocks, 0
    )
    present = local_pattern.astype(jnp.float32)
    masked = (
        owner_rows.reshape(local_blocks, BLOCK, col_blocks, BLOCK) * present[:, None, :, None]
    ).reshape(local_count, width)
    gathered = lax.all_gather(masked, "row", axis=0, tiled=True)
    strips = jnp.take(gathered.reshape(-1, BLOCK, width), targets.reshape(-1), axis=0).reshape(
        -1, width
    )
    update = product(masked, strips)
    empty = jnp.zeros_like(update)
    prior = carried_in(update, "col", combine, empty)
    carried = panels - prior - update
    return carried[None]


def solution(mesh):
    placed = (P("col", "row", None), P(), P(), P(), P("row", None))
    return jax.shard_map(
        body, mesh=mesh, in_specs=placed, out_specs=P("col", "row", None), check_vma=False
    )
```

profile of v0, /device:TPU:0, one launch (start us, length us, event | category | flops | bytes accessed | tf_op | source)
XLA Modules:
  0.0 108.5 jit_solution(18407228519424610172)
XLA Ops:
  6.5 0.0 all-gather.4.cloned.1.call-start
  6.5 1.3 %fusion.4 = s32[]{:T(128)} fusion(s32[8]{0:T(128)} %param.9, s32[]{:T(128)} %axis_index.27), kind=kLoop, calls=%fused_computation.17 | loop fusion | flops 23 | bytes 40 | tf_op jit(solution)/shard_map/reduce_sum | solution.py:43
  7.8 0.6 compare_convert_fusion
  8.5 0.8 multiply_reduce_fusion
  9.3 0.1 broadcast_bitcast_fusion
  9.4 1.9 %bitcast_multiply_fusion = f32[128,1024]{1,0:T(8,128)} fusion(f32[1,128,1024]{2,1,0:T(8,128)} %param.7, f32[1024]{0:T(1024)S(1)} %broadcast_bitcast_fusion), kind=kLoop, calls=%fused_computation.3 | loop fusion | flops 131072 | bytes 1052672 | tf_op jit(solution)/shard_map/mul | solution.py:53
  11.3 0.0 all-gather.4.cloned.1.call-update
  11.3 0.0 all-gather.6.cloned.1.call-start
  11.3 0.8 reshape.98
  12.1 0.8 reshape.96
  12.9 23.8 %all-gather.4.cloned.1.call-done = f32[512,1024]{1,0:T(8,128)} async-done(((f32[128,1024]{1,0:T(8,128)}), f32[512,1024]{1,0:T(8,128)}) %all-gather.4.cloned.1.call-update) | async-done | bytes 2097168 | tf_op jit(solution)/shard_map/all_gather | solution.py:55
  36.7 2.3 %gather_fusion = f32[4,128,1024]{2,1,0:T(8,128)S(1)} fusion(f32[4,128,1024]{2,1,0:T(8,128)} %bitcast.22, s32[1024]{0:T(1024)S(1)} %pad_clamp_fusion), kind=kCustom, calls=%fused_computation | custom fusion | bytes 4194320 | tf_op jit(solution)/shard_map/jit(_take)/gather | solution.py:56
  39.0 0.0 copy-start.1
  39.0 0.3 broadcast_select_fusion
  39.3 0.7 copy-done.1
  40.0 2.9 %fusion = f32[128,512]{1,0:T(8,128)} fusion(f32[512,1024]{1,0:T(8,128)S(1)} %bitcast.21, f32[1,128,1024]{2,1,0:T(8,128)S(1)} %copy-done.1, f32[1024]{0:T(1024)S(1)} %broadcast_bitcast_fusion), kind=kOutput, calls=%fused_computation.4 | convolution fusion | flops 805437440 | bytes 2887680 | tf_op jit(solution)/shard_map/dot_general | solution.py:23
  43.0 0.0 all-gather.6.cloned.1.call-update
  43.0 0.0 copy-start
  43.0 0.0 copy-start.2
  43.1 49.2 %all-gather.6.cloned.1.call-done = f32[1024,512]{1,0:T(8,128)} async-done(((f32[128,512]{1,0:T(8,128)}), f32[1024,512]{1,0:T(8,128)}) %all-gather.6.cloned.1.call-update) | async-done | bytes 2097168 | tf_op jit(solution)/shard_map/all_gather | solution.py:11
  92.3 8.6 %while.14 = (s32[]{:T(128)}, f32[128,512]{1,0:T(8,128)S(1)}, s32[]{:T(128)}, f32[8,128,512]{2,1,0:T(8,128)}, s32[]{:T(128)}, /*index=5*/s32[]{:T(128)}) while((s32[]{:T(128)}, f32[128,512]{1,0:T(8,128)S(1)}, s32[]{:T(128)}, f32[8,128,512]{2,1,0:T(8,128)}, s32[]{:T(128)}, /*index=5*/s32[]{:T(128)}) %tuple.39), condition=%wide.region_3.4_spmd.clone, body=%wide.region_2.3_spmd.clone.sunk | while | flops 196612 | bytes 786525 | solution.py:19
  92.3 1.0 add_select_fusion.2
  93.3 1.0 add_select_fusion.2
  94.4 1.0 add_select_fusion.2
  95.5 1.0 add_select_fusion.2
  96.6 1.0 add_select_fusion.2
  97.6 1.0 add_select_fusion.2
  98.7 1.0 add_select_fusion.2
  99.8 1.0 add_select_fusion.2
  100.8 0.0 copy-done
  100.9 0.0 copy-done.2
  100.9 0.8 subtract_bitcast_fusion
  (5 shorter events, 0.0 us)
Async XLA Ops:
  6.5 30.2 %all-gather.4.cloned.1.call-start = ((), (), s32[]{:S(2)}) async-start(), calls=%async_computation | async-start | bytes 2621440 | tf_op jit(solution)/shard_map/all_gather | solution.py:55
  11.3 81.0 %all-gather.6.cloned.1.call-start = ((), (), s32[]{:S(2)}) async-start(), calls=%async_computation.1 | async-start | bytes 2359296 | tf_op jit(solution)/shard_map/all_gather | solution.py:11
  39.0 1.0 copy-start.1
  43.0 57.8 %copy-start = (f32[128,512]{1,0:T(8,128)S(1)}, f32[128,512]{1,0:T(8,128)}, u32[]{:S(2)}) copy-start(f32[128,512]{1,0:T(8,128)} %fusion) | copy-start | bytes 786436
  43.0 57.8 %copy-start.2 = (f32[128,512]{1,0:T(8,128)S(1)}, f32[128,512]{1,0:T(8,128)}, u32[]{:S(2)}) copy-start(f32[128,512]{1,0:T(8,128)} %param.11) | copy-start | bytes 786436
Sparse Core Ops, SparseCore 0:
  11.4 25.2 all-gather.3
  43.1 49.0 all-gather.5
where the time goes:
time: 109 us; the launch traced here: 108 us
  waiting for transfers between devices  73.1 us (67%)
  other arithmetic  14.1 us (13%)
  between operations  13.5 us (12%)
  local copies, waits for them, and re-layouts  4.6 us (4%)
  matrix products  2.95 us (3%)
    all_gather x1, waiting for transfers between devices, carried_in(): everything = lax.all_gather(value, axis)  49.2 us
    all_gather x1, waiting for transfers between devices, body(): gathered = lax.all_gather(masked, 'row', axis=0, tiled=True)  23.8 us
    select_n x8, other arithmetic, step(): return jnp.where(reached, new, before)  8.39 us
    dot_general x1, matrix products, product(): lax.dot_general(masked, strips, (((1,), (1,)), ((), ())), precision=lax.P...  2.95 us
    gather x1, local copies, waits for them, and re-layouts, body(): jnp.take(gathered.reshape(-1, BLOCK, width), targets.reshape(-1), axis=0)  2.27 us
  transfers between devices with their start and end apart: 2, of which 2 were waited for; matrix products, arithmetic and copies ran while one was open for 1% of the time, Pallas kernels for 0%

commit v1 on v0

v1 whole, which is shorter than its diff:
```python
import functools

import jax
import jax.numpy as jnp
from jax import lax
from jax.experimental import pallas as pl
from jax.experimental.pallas import tpu as pltpu
from jax.sharding import PartitionSpec as P

BLOCK = 128
PARAMS = pltpu.CompilerParams(vmem_limit_bytes=8 << 20)
NT = (((1,), (1,)), ((), ()))


def halves(value):
    high = value.astype(jnp.bfloat16)
    return high, (value - high.astype(jnp.float32)).astype(jnp.bfloat16)


def product(left, right):
    dot = functools.partial(lax.dot_general, dimension_numbers=NT, preferred_element_type=jnp.float32)
    return dot(left[0], right[0]) + (dot(left[0], right[1]) + dot(left[1], right[0]))


def masked(ref, present_ref, row):
    columns = ref.shape[1] // BLOCK
    parts = []
    for k in range(columns):
        keep = present_ref[row, k].astype(jnp.float32)
        parts.append(ref[:, k * BLOCK : (k + 1) * BLOCK] * keep)
    return jnp.concatenate(parts, axis=1)


def near_kernel(present_ref, own_ref, sibling_ref, out_ref):
    row = lax.axis_index("row")
    own = halves(masked(own_ref, present_ref, row))
    sibling = halves(masked(sibling_ref, present_ref, row ^ 1))
    out_ref[0] = product(own, own)
    out_ref[1] = product(own, sibling)


def far_kernel(present_ref, own_ref, sibling_ref, across_ref, after_ref, mine_ref, theirs_ref):
    del after_ref
    row = lax.axis_index("row")
    own = halves(masked(own_ref, present_ref, row))
    sibling = halves(masked(sibling_ref, present_ref, row ^ 1))
    across = halves(masked(across_ref, present_ref, row ^ 2))
    mine_ref[...] = product(own, across)
    theirs_ref[...] = product(sibling, across)


def finish_kernel(bit, targets_ref, panels_ref, near_ref, near_in_ref, far_ref, far_in_ref, out_ref):
    row = lax.axis_index("row")
    upper = (lax.axis_index("col") & bit) != 0
    per_panel = targets_ref.shape[1]
    sums = [(near_ref, near_in_ref, 0), (near_ref, near_in_ref, 1), (far_ref, far_in_ref, 0), (far_ref, far_in_ref, 1)]
    for slot in range(targets_ref.shape[0] * per_panel):
        place = targets_ref[slot // per_panel, slot % per_panel] ^ row
        columns = slice(slot * BLOCK, (slot + 1) * BLOCK)
        for j, (inclusive, incoming, k) in enumerate(sums):

            @pl.when(place == j)
            def _():
                earlier = jnp.where(upper, incoming[k], jnp.zeros_like(incoming[k]))
                out_ref[:, columns] = panels_ref[:, columns] - (inclusive[k] + earlier)


def swapped(value, axis, bit):
    return lax.ppermute(value, axis, [(i, i ^ bit) for i in range(lax.axis_size(axis))])


def scanned(update):
    place, size = lax.axis_index("col"), lax.axis_size("col")
    inclusive, total, bit, totals = update, update, 1, [update]
    while bit * 2 < size:
        other = swapped(total, "col", bit)
        inclusive = inclusive + jnp.where((place & bit) != 0, other, 0.0)
        total = total + other
        totals.append(total)
        bit *= 2
    return inclusive, swapped(total, "col", bit), bit, totals


def body(factor, pattern, order, targets, panels):
    own = factor[0]
    rows, width = own.shape
    smem, vmem = pl.BlockSpec(memory_space=pltpu.SMEM), pl.BlockSpec(memory_space=pltpu.VMEM)
    f32 = jnp.float32
    across = swapped(own, "row", 2)
    sibling = swapped(own, "row", 1)
    supernode = lax.dynamic_index_in_dim(order, lax.axis_index("col"), 0, keepdims=False)
    present = lax.dynamic_index_in_dim(pattern, supernode, 0, keepdims=False)
    flops = 2 * 3 * rows * BLOCK * width
    near = pl.pallas_call(
        near_kernel,
        out_shape=jax.ShapeDtypeStruct((2, rows, BLOCK), f32),
        in_specs=[smem, vmem, vmem],
        out_specs=vmem,
        compiler_params=PARAMS,
        cost_estimate=pl.CostEstimate(flops=2 * flops, bytes_accessed=8 * rows * width, transcendentals=0),
    )(present, own, sibling)
    near_sum, near_in, bit, totals = scanned(near)
    mine, theirs = pl.pallas_call(
        far_kernel,
        out_shape=[jax.ShapeDtypeStruct((rows, BLOCK), f32)] * 2,
        in_specs=[smem, vmem, vmem, vmem, pl.BlockSpec(memory_space=pl.ANY)],
        out_specs=[vmem, vmem],
        compiler_params=PARAMS,
        cost_estimate=pl.CostEstimate(flops=2 * flops, bytes_accessed=12 * rows * width, transcendentals=0),
    )(present, own, sibling, across, totals[1])
    far = jnp.stack([mine, swapped(theirs, "row", 1)])
    far_sum, far_in, bit, _ = scanned(far)
    carried = pl.pallas_call(
        functools.partial(finish_kernel, bit),
        out_shape=jax.ShapeDtypeStruct(panels.shape, f32),
        in_specs=[smem, vmem, vmem, vmem, vmem, vmem],
        out_specs=vmem,
        compiler_params=PARAMS,
        cost_estimate=pl.CostEstimate(flops=0, bytes_accessed=16 * rows * panels.shape[1], transcendentals=0),
    )(targets, panels, near_sum, near_in, far_sum, far_in)
    return carried[None]


def solution(mesh):
    placed = (P("col", "row", None), P(), P(), P(), P("row", None))
    return jax.shard_map(
        body, mesh=mesh, in_specs=placed, out_specs=P("col", "row", None), check_vma=False
    )
```

time: 109 us -> 42.1 us (0.39)
  waiting for transfers between devices: 73.1 us -> 17.4 us
  starting transfers between devices: 0.04 us -> 15.6 us
  other arithmetic: 14.1 us -> 0.1 us
  between operations: 13.5 us -> 2.04 us
  Pallas kernels: 0 us -> 3.76 us
  matrix products: 2.95 us -> 0 us
  local copies, waits for them, and re-layouts: 4.6 us -> 2.97 us
    all_gather x2 -> x0, waiting for transfers between devices: 73.1 us -> none  [the longest x1 49.2 us: carried_in(): everything = lax.all_gather(value, axis)]
    ppermute x0 -> x9, waiting for transfers between devices: none -> 17.4 us  [swapped(): lax.ppermute(value, axis, [(i, i ^ bit) for i in range(lax.axis_size(axis...]
    ppermute x0 -> x9, starting transfers between devices: none -> 15.6 us  [swapped(): lax.ppermute(value, axis, [(i, i ^ bit) for i in range(lax.axis_size(axis...]
    select_n x10 -> x0, other arithmetic: 8.7 us -> none  [the longest x8 8.39 us: step(): return jnp.where(reached, new, before)]
    pallas_call x0 -> x3, Pallas kernels: none -> 3.76 us  [the longest x1 1.39 us: body(): pl.pallas_call(functools.partial(finish_kernel, bit), out_shape=jax.Shape...]
    dot_general x1 -> x0, matrix products: 2.95 us -> none  [product(): lax.dot_general(masked, strips, (((1,), (1,)), ((), ())), precision=lax.P...]
    gather x1 -> x0, local copies, waits for them, and re-layouts: 2.27 us -> none  [body(): jnp.take(gathered.reshape(-1, BLOCK, width), targets.reshape(-1), axis=0)]
    reduce_sum x2 -> x0, other arithmetic: 2.1 us -> none  [the longest x1 1.29 us: body(): jnp.sum(jnp.where(jnp.arange(chain_length, dtype=jnp.int32) == position,...]
  transfers between devices with their start and end apart: 2 -> 9, of which waited for: 2 -> 7; matrix products, arithmetic and copies ran while one was open for 1% -> 2% of each run, Pallas kernels for 0% -> 3%
where the time goes in v1:
time: 42.1 us; the launch traced here: 41.9 us
  waiting for transfers between devices  17.4 us (41%)
  starting transfers between devices  15.6 us (37%)
  Pallas kernels  3.76 us (9%)
  local copies, waits for them, and re-layouts  2.97 us (7%)
  between operations  2.04 us (5%)
    ppermute x9, waiting for transfers between devices, swapped(): lax.ppermute(value, axis, [(i, i ^ bit) for i in range(lax.axis_size(axis...  17.4 us
    ppermute x9, starting transfers between devices, swapped(): lax.ppermute(value, axis, [(i, i ^ bit) for i in range(lax.axis_size(axis...  15.6 us
    unnamed x12, local copies, waits for them, and re-layouts  2.38 us
    pallas_call x1, Pallas kernels, body(): pl.pallas_call(functools.partial(finish_kernel, bit), out_shape=jax.Shape...  1.39 us
    pallas_call x1, Pallas kernels, body(): pl.pallas_call(far_kernel, out_shape=[jax.ShapeDtypeStruct((rows, BLOCK),...  1.22 us
    pallas_call x1, Pallas kernels, body(): pl.pallas_call(near_kernel, out_shape=jax.ShapeDtypeStruct((2, rows, BLOC...  1.16 us
  transfers between devices with their start and end apart: 9, of which 7 were waited for; matrix products, arithmetic and copies ran while one was open for 2% of the time, Pallas kernels for 3%

profile of v1, /device:TPU:0, one launch (start us, length us, event | category | flops | bytes accessed | tf_op | source)
XLA Modules:
  0.0 41.9 jit_solution(3586874776009983447)
XLA Ops:
  0.0 0.0 copy-start
  0.0 0.5 %collective-permute-start = (f32[128,1024]{1,0:T(8,128)}, f32[128,1024]{1,0:T(8,128)S(1)}, u32[]{:S(2)}, u32[]{:S(2)}) collective-permute-start(f32[128,1024]{1,0:T(8,128)} %bitcast.7), channel_id=1, source_target_pairs={{0,1},{1,0},{2,3},{3,2},{4,5},{5,4},{6,7},{7,6},{8,9},{9,8},{10,11... | collective-permute-start | bytes 1572872 | tf_op jit(solution)/shard_map/ppermute | solution.py:69
  0.5 2.5 %collective-permute-start.4 = (f32[128,1024]{1,0:T(8,128)}, f32[128,1024]{1,0:T(8,128)S(1)}, u32[]{:S(2)}, u32[]{:S(2)}) collective-permute-start(f32[128,1024]{1,0:T(8,128)} %bitcast.8), channel_id=1, source_target_pairs={{0,2},{1,3},{2,0},{3,1},{4,6},{5,7},{6,4},{7,5},{8,10},{9,11},{10,... | collective-permute-start | bytes 1572872 | tf_op jit(solution)/shard_map/ppermute | solution.py:69
  3.0 0.0 copy-start.5
  3.0 0.7 %copy-done.5 = s32[8]{0:T(128)S(1)} copy-done((s32[8]{0:T(128)S(1)}, s32[8]{0:T(128)}, u32[]{:S(2)}) %copy-start.5) | copy-done | bytes 56
  3.7 0.6 %dynamic_slice.8 = s32[1]{0:T(128)} dynamic-slice(s32[8]{0:T(128)S(1)} %copy-done.5, s32[]{:T(128)S(6)} %select_n.30), dynamic_slice_sizes={1} | dynamic-slice | bytes 12 | tf_op jit(solution)/shard_map/jit(dynamic_index_in_dim)/dynamic_slice | solution.py:91
  6.2 0.0 copy-done
  6.2 0.0 collective-permute-done.sibling_ref
  6.3 0.0 copy-start.1
  6.3 1.0 %copy-done.1 = f32[1,128,1024]{2,1,0:T(8,128)S(1)} copy-done((f32[1,128,1024]{2,1,0:T(8,128)S(1)}, f32[1,128,1024]{2,1,0:T(8,128)}, u32[]{:S(2)}) %copy-start.1) | copy-done | bytes 524312
  7.3 0.0 copy-start.2
  7.3 1.2 %shard_map.55 = f32[2,128,128]{2,1,0:T(8,128)S(1)} custom-call(s32[4,8]{1,0:T(4,128)S(1)} %dynamic-slice_bitcast_fusion.present_ref, f32[128,1024]{1,0:T(8,128)S(1)} %bitcast.9, f32[128,1024]{1,0:T(8,128)S(1)} %collective-permute-done.sibling_ref), custom_call_target="tpu_custom_call" | custom-call | flops 201326592 | bytes 1048576 | tf_op jit(solution)/shard_map/pallas_call | solution.py:94
  8.5 1.6 %collective-permute-start.1 = (f32[2,128,128]{2,1,0:T(8,128)S(1)}, f32[2,128,128]{2,1,0:T(8,128)S(1)}, u32[]{:S(2)}, u32[]{:S(2)}) collective-permute-start(f32[2,128,128]{2,1,0:T(8,128)S(1)} %shard_map.55), channel_id=1, source_target_pairs={{0,4},{4,0},{8,12},{12,8},{16,20},{20,16},{24,28},{28,24},{1,5},{5... | collective-permute-start | bytes 393224 | tf_op jit(solution)/shard_map/ppermute | solution.py:69
  10.1 4.0 %collective-permute-done.1 = f32[2,128,128]{2,1,0:T(8,128)S(1)} collective-permute-done((f32[2,128,128]{2,1,0:T(8,128)S(1)}, f32[2,128,128]{2,1,0:T(8,128)S(1)}, u32[]{:S(2)}, u32[]{:S(2)}) %collective-permute-start.1) | collective-permute-done | bytes 131104 | tf_op jit(solution)/shard_map/ppermute | solution.py:69
  14.1 1.7 %collective-permute-done.4.across_ref = f32[128,1024]{1,0:T(8,128)S(1)} collective-permute-done((f32[128,1024]{1,0:T(8,128)}, f32[128,1024]{1,0:T(8,128)S(1)}, u32[]{:S(2)}, u32[]{:S(2)}) %collective-permute-start.4) | collective-permute-done | bytes 524320 | tf_op jit(solution)/shard_map/ppermute | solution.py:69
  15.8 0.0 copy-done.2
  15.8 1.2 %shard_map.56 = (f32[128,128]{1,0:T(8,128)S(1)}, f32[128,128]{1,0:T(8,128)S(1)}) custom-call(s32[4,8]{1,0:T(4,128)S(1)} %dynamic-slice_bitcast_fusion.present_ref, f32[128,1024]{1,0:T(8,128)S(1)} %bitcast.10, f32[128,1024]{1,0:T(8,128)S(1)} %collective-permute-done.sibling_ref, f32[128,1024]{1,0:T(8,128)S(1)} %collective-permute-done.4.across_ref, ...), custom_call_target="tpu_custom_call" | custom-call | flops 201326592 | bytes 1572864 | tf_op jit(solution)/shard_map/pallas_call | solution.py:103
  17.0 0.1 collective-permute-start.5
  17.1 1.2 %collective-permute-done.5 = f32[128,128]{1,0:T(8,128)S(1)} collective-permute-done((f32[128,128]{1,0:T(8,128)S(1)}, f32[128,128]{1,0:T(8,128)S(1)}, u32[]{:S(2)}, u32[]{:S(2)}) %collective-permute-start.5) | collective-permute-done | bytes 65568 | tf_op jit(solution)/shard_map/ppermute | solution.py:69
  18.3 1.8 %collective-permute-start.6 = (f32[2,128,128]{2,1,0:T(8,128)S(1)}, f32[2,128,128]{2,1,0:T(8,128)S(1)}, u32[]{:S(2)}, u32[]{:S(2)}) collective-permute-start(f32[2,128,128]{2,1,0:T(8,128)S(1)} %pad_maximum_fusion), channel_id=1, source_target_pairs={{0,4},{4,0},{8,12},{12,8},{16,20},{20,16},{24,28},{28,24},{1,5},{5... | collective-permute-start | bytes 393224 | tf_op jit(solution)/shard_map/ppermute | solution.py:69
  20.2 1.6 %collective-permute-start.2 = (f32[2,128,128]{2,1,0:T(8,128)S(1)}, f32[2,128,128]{2,1,0:T(8,128)S(1)}, u32[]{:S(2)}, u32[]{:S(2)}) collective-permute-start(f32[2,128,128]{2,1,0:T(8,128)S(1)} %add.35.after_ref), channel_id=1, source_target_pairs={{0,8},{4,12},{8,0},{12,4},{16,24},{20,28},{24,16},{28,20},{1,9},{5... | collective-permute-start | bytes 393224 | tf_op jit(solution)/shard_map/ppermute | solution.py:69
  21.8 2.2 %collective-permute-done.6 = f32[2,128,128]{2,1,0:T(8,128)S(1)} collective-permute-done((f32[2,128,128]{2,1,0:T(8,128)S(1)}, f32[2,128,128]{2,1,0:T(8,128)S(1)}, u32[]{:S(2)}, u32[]{:S(2)}) %collective-permute-start.6) | collective-permute-done | bytes 131104 | tf_op jit(solution)/shard_map/ppermute | solution.py:69
  24.0 1.9 %collective-permute-start.7 = (f32[2,128,128]{2,1,0:T(8,128)S(1)}, f32[2,128,128]{2,1,0:T(8,128)S(1)}, u32[]{:S(2)}, u32[]{:S(2)}) collective-permute-start(f32[2,128,128]{2,1,0:T(8,128)S(1)} %fusion), channel_id=1, source_target_pairs={{0,8},{4,12},{8,0},{12,4},{16,24},{20,28},{24,16},{28,20},{1,9},{5... | collective-permute-start | bytes 393224 | tf_op jit(solution)/shard_map/ppermute | solution.py:69
  25.9 0.0 collective-permute-done.2
  25.9 0.0 copy-start.3
  25.9 2.6 %collective-permute-start.3 = (f32[2,128,128]{2,1,0:T(8,128)S(1)}, f32[2,128,128]{2,1,0:T(8,128)S(1)}, u32[]{:S(2)}, u32[]{:S(2)}) collective-permute-start(f32[2,128,128]{2,1,0:T(8,128)S(1)} %get-tuple-element.11), channel_id=1, source_target_pairs={{0,16},{4,20},{8,24},{12,28},{16,0},{20,4},{24,8},{28,12},{1,17},{... | collective-permute-start | bytes 393224 | tf_op jit(solution)/shard_map/ppermute | solution.py:69
  28.6 1.8 %collective-permute-done.7 = f32[2,128,128]{2,1,0:T(8,128)S(1)} collective-permute-done((f32[2,128,128]{2,1,0:T(8,128)S(1)}, f32[2,128,128]{2,1,0:T(8,128)S(1)}, u32[]{:S(2)}, u32[]{:S(2)}) %collective-permute-start.7) | collective-permute-done | bytes 131104 | tf_op jit(solution)/shard_map/ppermute | solution.py:69
  30.4 3.0 %collective-permute-start.8 = (f32[2,128,128]{2,1,0:T(8,128)S(1)}, f32[2,128,128]{2,1,0:T(8,128)S(1)}, u32[]{:S(2)}, u32[]{:S(2)}) collective-permute-start(f32[2,128,128]{2,1,0:T(8,128)S(1)} %get-tuple-element.9), channel_id=1, source_target_pairs={{0,16},{4,20},{8,24},{12,28},{16,0},{20,4},{24,8},{28,12},{1,17},{... | collective-permute-start | bytes 393224 | tf_op jit(solution)/shard_map/ppermute | solution.py:69
  33.4 4.8 %collective-permute-done.3.near_in_ref = f32[2,128,128]{2,1,0:T(8,128)S(1)} collective-permute-done((f32[2,128,128]{2,1,0:T(8,128)S(1)}, f32[2,128,128]{2,1,0:T(8,128)S(1)}, u32[]{:S(2)}, u32[]{:S(2)}) %collective-permute-start.3) | collective-permute-done | bytes 131104 | tf_op jit(solution)/shard_map/ppermute | solution.py:69
  38.2 1.6 %collective-permute-done.8.far_in_ref = f32[2,128,128]{2,1,0:T(8,128)S(1)} collective-permute-done((f32[2,128,128]{2,1,0:T(8,128)S(1)}, f32[2,128,128]{2,1,0:T(8,128)S(1)}, u32[]{:S(2)}, u32[]{:S(2)}) %collective-permute-start.8) | collective-permute-done | bytes 131104 | tf_op jit(solution)/shard_map/ppermute | solution.py:69
  39.8 0.0 copy-start.4
  39.8 0.0 copy-done.3
  39.8 0.7 %copy-done.4 = s32[2,2]{1,0:T(2,128)S(1)} copy-done((s32[2,2]{1,0:T(2,128)S(1)}, s32[2,2]{1,0:T(2,128)}, u32[]{:S(2)}) %copy-start.4) | copy-done | bytes 40
  40.5 1.4 %shard_map.57 = f32[128,512]{1,0:T(8,128)} custom-call(s32[2,2]{1,0:T(2,128)S(1)} %copy-done.4, f32[128,512]{1,0:T(8,128)S(1)} %copy-done.3, f32[2,128,128]{2,1,0:T(8,128)S(1)} %get-tuple-element.12.near_ref, f32[2,128,128]{2,1,0:T(8,128)S(1)} %collective-permute-done.3.near_in_ref, f32[2,128,128]{2,1,0:T(8,128)S(1)} %get-tuple-element.10.far_ref, ...), custom_call_target="tpu_custom_call" | custom-call | bytes 1048576 | tf_op jit(solution)/shard_map/pallas_call | solution.py:113
  (6 shorter events, 0.1 us)
Async XLA Ops:
  0.0 6.2 %copy-start = (s32[8,4,8]{2,1,0:T(4,128)S(1)}, s32[8,4,8]{2,1,0:T(4,128)}, u32[]{:S(2)}) copy-start(s32[8,4,8]{2,1,0:T(4,128)} %param.6) | copy-start | bytes 3076
  0.0 6.2 %collective-permute-start = (f32[128,1024]{1,0:T(8,128)}, f32[128,1024]{1,0:T(8,128)S(1)}, u32[]{:S(2)}, u32[]{:S(2)}) collective-permute-start(f32[128,1024]{1,0:T(8,128)} %bitcast.7), channel_id=1, source_target_pairs={{0,1},{1,0},{2,3},{3,2},{4,5},{5,4},{6,7},{7,6},{8,9},{9,8},{10,11... | collective-permute-start | bytes 1572872 | tf_op jit(solution)/shard_map/ppermute | solution.py:69
  0.5 15.3 %collective-permute-start.4 = (f32[128,1024]{1,0:T(8,128)}, f32[128,1024]{1,0:T(8,128)S(1)}, u32[]{:S(2)}, u32[]{:S(2)}) collective-permute-start(f32[128,1024]{1,0:T(8,128)} %bitcast.8), channel_id=1, source_target_pairs={{0,2},{1,3},{2,0},{3,1},{4,6},{5,7},{6,4},{7,5},{8,10},{9,11},{10,... | collective-permute-start | bytes 1572872 | tf_op jit(solution)/shard_map/ppermute | solution.py:69
  3.0 0.7 %copy-start.5 = (s32[8]{0:T(128)S(1)}, s32[8]{0:T(128)}, u32[]{:S(2)}) copy-start(s32[8]{0:T(128)} %param.7) | copy-start | bytes 100
  6.3 1.0 %copy-start.1 = (f32[1,128,1024]{2,1,0:T(8,128)S(1)}, f32[1,128,1024]{2,1,0:T(8,128)}, u32[]{:S(2)}) copy-start(f32[1,128,1024]{2,1,0:T(8,128)} %param.5) | copy-start | bytes 1572868
  7.3 8.5 %copy-start.2 = (f32[1,128,1024]{2,1,0:T(8,128)S(1)}, f32[1,128,1024]{2,1,0:T(8,128)}, u32[]{:S(2)}) copy-start(f32[1,128,1024]{2,1,0:T(8,128)} %param.5) | copy-start | bytes 1572868
  8.5 5.6 %collective-permute-start.1 = (f32[2,128,128]{2,1,0:T(8,128)S(1)}, f32[2,128,128]{2,1,0:T(8,128)S(1)}, u32[]{:S(2)}, u32[]{:S(2)}) collective-permute-start(f32[2,128,128]{2,1,0:T(8,128)S(1)} %shard_map.55), channel_id=1, source_target_pairs={{0,4},{4,0},{8,12},{12,8},{16,20},{20,16},{24,28},{28,24},{1,5},{5... | collective-permute-start | bytes 393224 | tf_op jit(solution)/shard_map/ppermute | solution.py:69
  17.0 1.3 %collective-permute-start.5 = (f32[128,128]{1,0:T(8,128)S(1)}, f32[128,128]{1,0:T(8,128)S(1)}, u32[]{:S(2)}, u32[]{:S(2)}) collective-permute-start(f32[128,128]{1,0:T(8,128)S(1)} %get-tuple-element.8), channel_id=1, source_target_pairs={{0,1},{1,0},{2,3},{3,2},{4,5},{5,4},{6,7},{7,6},{8,9},{9,8},{10,11... | collective-permute-start | bytes 196616 | tf_op jit(solution)/shard_map/ppermute | solution.py:69
  18.3 5.7 %collective-permute-start.6 = (f32[2,128,128]{2,1,0:T(8,128)S(1)}, f32[2,128,128]{2,1,0:T(8,128)S(1)}, u32[]{:S(2)}, u32[]{:S(2)}) collective-permute-start(f32[2,128,128]{2,1,0:T(8,128)S(1)} %pad_maximum_fusion), channel_id=1, source_target_pairs={{0,4},{4,0},{8,12},{12,8},{16,20},{20,16},{24,28},{28,24},{1,5},{5... | collective-permute-start | bytes 393224 | tf_op jit(solution)/shard_map/ppermute | solution.py:69
  20.2 5.7 %collective-permute-start.2 = (f32[2,128,128]{2,1,0:T(8,128)S(1)}, f32[2,128,128]{2,1,0:T(8,128)S(1)}, u32[]{:S(2)}, u32[]{:S(2)}) collective-permute-start(f32[2,128,128]{2,1,0:T(8,128)S(1)} %add.35.after_ref), channel_id=1, source_target_pairs={{0,8},{4,12},{8,0},{12,4},{16,24},{20,28},{24,16},{28,20},{1,9},{5... | collective-permute-start | bytes 393224 | tf_op jit(solution)/shard_map/ppermute | solution.py:69
  24.0 6.3 %collective-permute-start.7 = (f32[2,128,128]{2,1,0:T(8,128)S(1)}, f32[2,128,128]{2,1,0:T(8,128)S(1)}, u32[]{:S(2)}, u32[]{:S(2)}) collective-permute-start(f32[2,128,128]{2,1,0:T(8,128)S(1)} %fusion), channel_id=1, source_target_pairs={{0,8},{4,12},{8,0},{12,4},{16,24},{20,28},{24,16},{28,20},{1,9},{5... | collective-permute-start | bytes 393224 | tf_op jit(solution)/shard_map/ppermute | solution.py:69
  25.9 13.9 %copy-start.3 = (f32[128,512]{1,0:T(8,128)S(1)}, f32[128,512]{1,0:T(8,128)}, u32[]{:S(2)}) copy-start(f32[128,512]{1,0:T(8,128)} %panels_ref.1) | copy-start | bytes 786436
  25.9 12.2 %collective-permute-start.3 = (f32[2,128,128]{2,1,0:T(8,128)S(1)}, f32[2,128,128]{2,1,0:T(8,128)S(1)}, u32[]{:S(2)}, u32[]{:S(2)}) collective-permute-start(f32[2,128,128]{2,1,0:T(8,128)S(1)} %get-tuple-element.11), channel_id=1, source_target_pairs={{0,16},{4,20},{8,24},{12,28},{16,0},{20,4},{24,8},{28,12},{1,17},{... | collective-permute-start | bytes 393224 | tf_op jit(solution)/shard_map/ppermute | solution.py:69
  30.4 9.4 %collective-permute-start.8 = (f32[2,128,128]{2,1,0:T(8,128)S(1)}, f32[2,128,128]{2,1,0:T(8,128)S(1)}, u32[]{:S(2)}, u32[]{:S(2)}) collective-permute-start(f32[2,128,128]{2,1,0:T(8,128)S(1)} %get-tuple-element.9), channel_id=1, source_target_pairs={{0,16},{4,20},{8,24},{12,28},{16,0},{20,4},{24,8},{28,12},{1,17},{... | collective-permute-start | bytes 393224 | tf_op jit(solution)/shard_map/ppermute | solution.py:69
  39.8 0.7 %copy-start.4 = (s32[2,2]{1,0:T(2,128)S(1)}, s32[2,2]{1,0:T(2,128)}, u32[]{:S(2)}) copy-start(s32[2,2]{1,0:T(2,128)} %targets_ref.1) | copy-start | bytes 52

commit v2 on v1

v2 whole, which is shorter than its diff:
```python
import functools

import jax
import jax.numpy as jnp
from jax import lax
from jax.experimental import pallas as pl
from jax.experimental.pallas import tpu as pltpu
from jax.sharding import PartitionSpec as P


BLOCK = 128
PARAMS = pltpu.CompilerParams(vmem_limit_bytes=8 << 20)
NT = (((1,), (1,)), ((), ()))
SMEM = pl.BlockSpec(memory_space=pltpu.SMEM)
VMEM = pl.BlockSpec(memory_space=pltpu.VMEM)
F32, BF16 = jnp.float32, jnp.bfloat16


def halves(value):
    high = value.astype(BF16)
    return high, (value - high.astype(F32)).astype(BF16)


def product(left, right):
    dot = functools.partial(lax.dot_general, dimension_numbers=NT, preferred_element_type=F32)
    return dot(left[0], right[0]) + (dot(left[0], right[1]) + dot(left[1], right[0]))


def masked(ref, present_ref, row):
    parts = []
    for k in range(ref.shape[1] // BLOCK):
        keep = present_ref[row, k].astype(F32)
        parts.append(ref[:, k * BLOCK : (k + 1) * BLOCK] * keep)
    return jnp.concatenate(parts, axis=1)


def near_kernel(order_ref, pattern_ref, own_ref, sibling_ref, out_ref, high_ref, low_ref, present_ref):
    row = lax.axis_index("row")
    supernode = order_ref[lax.axis_index("col")]
    for i in range(pattern_ref.shape[1]):
        for k in range(pattern_ref.shape[2]):
            present_ref[i, k] = pattern_ref[supernode, i, k]
    own = halves(masked(own_ref, present_ref, row))
    sibling = halves(masked(sibling_ref, present_ref, row ^ 1))
    out_ref[0] = product(own, own)
    out_ref[1] = product(own, sibling)
    for kept, mine, theirs in zip((high_ref, low_ref), own, sibling, strict=True):
        kept[...] = jnp.where((row & 2) == 0, mine, theirs)


def far_kernel(present_ref, high_ref, low_ref, across_ref, out_ref):
    across = halves(masked(across_ref, present_ref, lax.axis_index("row") ^ 2))
    out_ref[...] = product(across, (high_ref[...], low_ref[...]))


def finish_kernel(bit, targets_ref, panels_ref, near_ref, near_in_ref, own_ref, across_ref, sibling_ref, out_ref):
    row = lax.axis_index("row")
    upper = (lax.axis_index("col") & bit) != 0
    first = (row & 2) == 0
    slots = range(targets_ref.shape[0] * targets_ref.shape[1])

    def place(j, value):
        for slot in slots:
            columns = slice(slot * BLOCK, (slot + 1) * BLOCK)

            @pl.when((targets_ref[slot // targets_ref.shape[1], slot % targets_ref.shape[1]] ^ row) == j)
            def _():
                out_ref[:, columns] = panels_ref[:, columns] - value

    for j in range(2):
        earlier = jnp.where(upper, near_in_ref[j], jnp.zeros_like(near_in_ref[j]))
        place(j, near_ref[j] + earlier)
    turned = jnp.where(first, own_ref[...], sibling_ref[...]).T
    straight = across_ref[...]
    place(2, jnp.where(first, turned, straight))
    place(3, jnp.where(first, straight, turned))


def swapped(value, axis, bit):
    return lax.ppermute(value, axis, [(i, i ^ bit) for i in range(lax.axis_size(axis))])


def scanned(update):
    place, size = lax.axis_index("col"), lax.axis_size("col")
    inclusive, total, bit = update, update, 1
    while bit * 2 < size:
        other = swapped(total, "col", bit)
        inclusive = inclusive + jnp.where((place & bit) != 0, other, 0.0)
        total = total + other
        bit = bit * 2
    return inclusive, swapped(total, "col", bit), bit


def kernel(call, **kwargs):
    def run(*args):
        return pl.pallas_call(call, compiler_params=PARAMS, **kwargs)(*args)

    return run


def body(factor, pattern, order, targets, panels):
    own = factor[0]
    rows, width = own.shape
    sibling = swapped(own, "row", 1)
    across = swapped(own, "row", 2)
    flops = 2 * 3 * rows * BLOCK * width
    near, high, low, present = kernel(
        near_kernel,
        out_shape=[
            jax.ShapeDtypeStruct((2, rows, BLOCK), F32),
            jax.ShapeDtypeStruct((rows, width), BF16),
            jax.ShapeDtypeStruct((rows, width), BF16),
            jax.ShapeDtypeStruct(pattern.shape[1:], jnp.int32),
        ],
        in_specs=[SMEM, SMEM, VMEM, VMEM],
        out_specs=[VMEM, VMEM, VMEM, SMEM],
        cost_estimate=pl.CostEstimate(flops=2 * flops, bytes_accessed=12 * rows * width, transcendentals=0),
    )(order, pattern, own, sibling)
    near_sum, near_in, bit = scanned(near)
    far = kernel(
        far_kernel,
        out_shape=jax.ShapeDtypeStruct((rows, rows), F32),
        in_specs=[SMEM, VMEM, VMEM, VMEM],
        out_specs=VMEM,
        cost_estimate=pl.CostEstimate(flops=flops, bytes_accessed=8 * rows * width, transcendentals=0),
    )(present, high, low, across)
    far_sum, far_in, bit = scanned(far)
    mine = far_sum + jnp.where((lax.axis_index("col") & bit) != 0, far_in, 0.0)
    theirs, beside = swapped(mine, "row", 2), swapped(mine, "row", 1)
    carried = kernel(
        functools.partial(finish_kernel, bit),
        out_shape=jax.ShapeDtypeStruct(panels.shape, F32),
        in_specs=[SMEM] + [VMEM] * 6,
        out_specs=VMEM,
        cost_estimate=pl.CostEstimate(flops=0, bytes_accessed=16 * rows * panels.shape[1], transcendentals=0),
    )(targets, panels, near_sum, near_in, mine, theirs, beside)
    return carried[None]


def solution(mesh):
    placed = (P("col", "row", None), P(), P(), P(), P("row", None))
    return jax.shard_map(
        body, mesh=mesh, in_specs=placed, out_specs=P("col", "row", None), check_vma=False
    )
```

time: 42.1 us -> 39.6 us (0.941)
  between operations: 2.04 us -> 0.08 us
  local copies, waits for them, and re-layouts: 2.97 us -> 1.8 us
  waiting for transfers between devices: 17.4 us -> 18 us
    ppermute x9 -> x10, waiting for transfers between devices: 17.4 us -> 18 us  [swapped(): lax.ppermute(value, axis, [(i, i ^ bit) for i in range(lax.axis_size(axis...]
    dynamic_slice x1 -> x0, local copies, waits for them, and re-layouts: 0.58 us -> none  [body(): lax.dynamic_index_in_dim(order, lax.axis_index('col'), 0, keepdims=False)]
    unnamed x12 -> x10, local copies, waits for them, and re-layouts: 2.38 us -> 1.8 us
    ppermute x9 -> x10, starting transfers between devices: 15.6 us -> 15.4 us  [swapped(): lax.ppermute(value, axis, [(i, i ^ bit) for i in range(lax.axis_size(axis...]
  transfers between devices with their start and end apart: 9 -> 10, of which waited for: 7 -> 5; matrix products, arithmetic and copies ran while one was open for 2% -> 0% of each run, Pallas kernels for 3% -> 6%
where the time goes in v2:
time: 39.6 us; the launch traced here: 39.3 us
  waiting for transfers between devices  18 us (45%)
  starting transfers between devices  15.4 us (39%)
  Pallas kernels  3.99 us (10%)
  local copies, waits for them, and re-layouts  1.8 us (5%)
    ppermute x10, waiting for transfers between devices, swapped(): lax.ppermute(value, axis, [(i, i ^ bit) for i in range(lax.axis_size(axis...  18 us
    ppermute x10, starting transfers between devices, swapped(): lax.ppermute(value, axis, [(i, i ^ bit) for i in range(lax.axis_size(axis...  15.4 us
    pallas_call x3, Pallas kernels, run(): return pl.pallas_call(call, compiler_params=PARAMS, **kwargs)(*args)  3.99 us
    unnamed x10, local copies, waits for them, and re-layouts  1.8 us
  transfers between devices with their start and end apart: 10, of which 5 were waited for; matrix products, arithmetic and copies ran while one was open for 0% of the time, Pallas kernels for 6%

profile of v2, /device:TPU:0, one launch (start us, length us, event | category | flops | bytes accessed | tf_op | source)
XLA Modules:
  0.0 39.3 jit_solution(16271855451639380784)
XLA Ops:
  0.0 0.0 copy-start.4
  0.0 0.5 %collective-permute-start = (f32[128,1024]{1,0:T(8,128)}, f32[128,1024]{1,0:T(8,128)S(1)}, u32[]{:S(2)}, u32[]{:S(2)}) collective-permute-start(f32[128,1024]{1,0:T(8,128)} %bitcast.2), channel_id=1, source_target_pairs={{0,1},{1,0},{2,3},{3,2},{4,5},{5,4},{6,7},{7,6},{8,9},{9,8},{10,11... | collective-permute-start | bytes 1572872 | tf_op jit(solution)/shard_map/ppermute | solution.py:80
  0.5 2.5 %collective-permute-start.4 = (f32[128,1024]{1,0:T(8,128)}, f32[128,1024]{1,0:T(8,128)S(1)}, u32[]{:S(2)}, u32[]{:S(2)}) collective-permute-start(f32[128,1024]{1,0:T(8,128)} %bitcast.3), channel_id=1, source_target_pairs={{0,2},{1,3},{2,0},{3,1},{4,6},{5,7},{6,4},{7,5},{8,10},{9,11},{10,... | collective-permute-start | bytes 1572872 | tf_op jit(solution)/shard_map/ppermute | solution.py:80
  3.0 0.0 collective-permute-done.sibling_ref
  3.0 0.0 copy-done.4
  3.0 0.0 copy-start
  3.0 1.1 %copy-done = f32[1,128,1024]{2,1,0:T(8,128)S(1)} copy-done((f32[1,128,1024]{2,1,0:T(8,128)S(1)}, f32[1,128,1024]{2,1,0:T(8,128)}, u32[]{:S(2)}) %copy-start) | copy-done | bytes 524312
  4.1 0.0 copy-start.2
  4.1 0.7 %copy-done.2 = s32[8,4,8]{2,1,0:T(4,128)S(1)} copy-done((s32[8,4,8]{2,1,0:T(4,128)S(1)}, s32[8,4,8]{2,1,0:T(4,128)}, u32[]{:S(2)}) %copy-start.2) | copy-done | bytes 1048
  4.8 1.5 %shard_map.55 = (f32[2,128,128]{2,1,0:T(8,128)S(1)}, bf16[128,1024]{1,0:T(8,128)(2,1)S(1)}, bf16[128,1024]{1,0:T(8,128)(2,1)S(1)}, s32[4,8]{1,0:T(4,128)S(1)}) custom-call(s32[8]{0:T(128)S(1)} %copy-done.4, s32[8,4,8]{2,1,0:T(4,128)S(1)} %copy-done.2, f32[128,1024]{1,0:T(8,128)S(1)} %bitcast.4, f32[128,1024]{1,0:T(8,128)S(1)} %collective-permute-done.sibling_ref), custom_call_target="tpu_custom_call" | custom-call | flops 201326592 | bytes 1572864 | tf_op jit(solution)/shard_map/pallas_call | solution.py:96
  6.4 2.1 %collective-permute-start.1 = (f32[2,128,128]{2,1,0:T(8,128)S(1)}, f32[2,128,128]{2,1,0:T(8,128)S(1)}, u32[]{:S(2)}, u32[]{:S(2)}) collective-permute-start(f32[2,128,128]{2,1,0:T(8,128)S(1)} %get-tuple-element.9), channel_id=1, source_target_pairs={{0,4},{4,0},{8,12},{12,8},{16,20},{20,16},{24,28},{28,24},{1,5},{5... | collective-permute-start | bytes 393224 | tf_op jit(solution)/shard_map/ppermute | solution.py:80
  8.5 7.3 %collective-permute-done.4.across_ref = f32[128,1024]{1,0:T(8,128)S(1)} collective-permute-done((f32[128,1024]{1,0:T(8,128)}, f32[128,1024]{1,0:T(8,128)S(1)}, u32[]{:S(2)}, u32[]{:S(2)}) %collective-permute-start.4) | collective-permute-done | bytes 524320 | tf_op jit(solution)/shard_map/ppermute | solution.py:80
  15.8 0.9 %shard_map.56 = f32[128,128]{1,0:T(8,128)S(1)} custom-call(s32[4,8]{1,0:T(4,128)S(1)} %get-tuple-element.10.present_ref, bf16[128,1024]{1,0:T(8,128)(2,1)S(1)} %get-tuple-element.11.high_ref, bf16[128,1024]{1,0:T(8,128)(2,1)S(1)} %get-tuple-element.12.low_ref, f32[128,1024]{1,0:T(8,128)S(1)} %collective-permute-done.4.across_ref), custom_call_target="tpu_custom_call" | custom-call | flops 100663296 | bytes 1048576 | tf_op jit(solution)/shard_map/pallas_call | solution.py:96
  16.7 1.8 %collective-permute-start.5 = (f32[128,128]{1,0:T(8,128)S(1)}, f32[128,128]{1,0:T(8,128)S(1)}, u32[]{:S(2)}, u32[]{:S(2)}) collective-permute-start(f32[128,128]{1,0:T(8,128)S(1)} %shard_map.56), channel_id=1, source_target_pairs={{0,4},{4,0},{8,12},{12,8},{16,20},{20,16},{24,28},{28,24},{1,5},{5... | collective-permute-start | bytes 196616 | tf_op jit(solution)/shard_map/ppermute | solution.py:80
  18.6 0.0 collective-permute-done.1
  18.6 1.6 %collective-permute-start.2 = (f32[2,128,128]{2,1,0:T(8,128)S(1)}, f32[2,128,128]{2,1,0:T(8,128)S(1)}, u32[]{:S(2)}, u32[]{:S(2)}) collective-permute-start(f32[2,128,128]{2,1,0:T(8,128)S(1)} %add.28), channel_id=1, source_target_pairs={{0,8},{4,12},{8,0},{12,4},{16,24},{20,28},{24,16},{28,20},{1,9},{5... | collective-permute-start | bytes 393224 | tf_op jit(solution)/shard_map/ppermute | solution.py:80
  20.2 0.8 %collective-permute-done.5 = f32[128,128]{1,0:T(8,128)S(1)} collective-permute-done((f32[128,128]{1,0:T(8,128)S(1)}, f32[128,128]{1,0:T(8,128)S(1)}, u32[]{:S(2)}, u32[]{:S(2)}) %collective-permute-start.5) | collective-permute-done | bytes 65568 | tf_op jit(solution)/shard_map/ppermute | solution.py:80
  21.1 1.9 %collective-permute-start.6 = (f32[128,128]{1,0:T(8,128)S(1)}, f32[128,128]{1,0:T(8,128)S(1)}, u32[]{:S(2)}, u32[]{:S(2)}) collective-permute-start(f32[128,128]{1,0:T(8,128)S(1)} %add.32), channel_id=1, source_target_pairs={{0,8},{4,12},{8,0},{12,4},{16,24},{20,28},{24,16},{28,20},{1,9},{5... | collective-permute-start | bytes 196616 | tf_op jit(solution)/shard_map/ppermute | solution.py:80
  23.0 2.4 %collective-permute-done.6 = f32[128,128]{1,0:T(8,128)S(1)} collective-permute-done((f32[128,128]{1,0:T(8,128)S(1)}, f32[128,128]{1,0:T(8,128)S(1)}, u32[]{:S(2)}, u32[]{:S(2)}) %collective-permute-start.6) | collective-permute-done | bytes 65568 | tf_op jit(solution)/shard_map/ppermute | solution.py:80
  25.4 2.9 %collective-permute-start.7 = (f32[128,128]{1,0:T(8,128)S(1)}, f32[128,128]{1,0:T(8,128)S(1)}, u32[]{:S(2)}, u32[]{:S(2)}) collective-permute-start(f32[128,128]{1,0:T(8,128)S(1)} %add.34), channel_id=1, source_target_pairs={{0,16},{4,20},{8,24},{12,28},{16,0},{20,4},{24,8},{28,12},{1,17},{... | collective-permute-start | bytes 196616 | tf_op jit(solution)/shard_map/ppermute | solution.py:80
  28.3 0.0 collective-permute-done.2
  28.4 0.0 copy-start.1
  28.4 0.1 collective-permute-start.3
  28.5 4.9 %collective-permute-done.7 = f32[128,128]{1,0:T(8,128)S(1)} collective-permute-done((f32[128,128]{1,0:T(8,128)S(1)}, f32[128,128]{1,0:T(8,128)S(1)}, u32[]{:S(2)}, u32[]{:S(2)}) %collective-permute-start.7) | collective-permute-done | bytes 65568 | tf_op jit(solution)/shard_map/ppermute | solution.py:80
  33.5 0.0 copy-start.3
  33.5 1.8 %collective-permute-start.8 = (f32[128,128]{1,0:T(8,128)S(1)}, f32[128,128]{1,0:T(8,128)S(1)}, u32[]{:S(2)}, u32[]{:S(2)}) collective-permute-start(f32[128,128]{1,0:T(8,128)S(1)} %select_add_fusion.1.own_ref), channel_id=1, source_target_pairs={{0,2},{1,3},{2,0},{3,1},{4,6},{5,7},{6,4},{7,5},{8,10},{9,11},{10,... | collective-permute-start | bytes 196616 | tf_op jit(solution)/shard_map/ppermute | solution.py:80
  35.3 0.0 collective-permute-start.9
  35.3 2.5 %collective-permute-done.8.across_ref = f32[128,128]{1,0:T(8,128)S(1)} collective-permute-done((f32[128,128]{1,0:T(8,128)S(1)}, f32[128,128]{1,0:T(8,128)S(1)}, u32[]{:S(2)}, u32[]{:S(2)}) %collective-permute-start.8) | collective-permute-done | bytes 65568 | tf_op jit(solution)/shard_map/ppermute | solution.py:80
  37.8 0.0 collective-permute-done.9.sibling_ref
  37.8 0.0 collective-permute-done.3.near_in_ref
  37.8 0.0 copy-done.1
  37.8 0.0 copy-done.3
  37.8 1.5 %shard_map.57 = f32[128,512]{1,0:T(8,128)} custom-call(s32[2,2]{1,0:T(2,128)S(1)} %copy-done.3, f32[128,512]{1,0:T(8,128)S(1)} %copy-done.1, f32[2,128,128]{2,1,0:T(8,128)S(1)} %get-tuple-element.14.near_ref, f32[2,128,128]{2,1,0:T(8,128)S(1)} %collective-permute-done.3.near_in_ref, f32[128,128]{1,0:T(8,128)S(1)} %select_add_fusion.1.own_ref, ...), custom_call_target="tpu_custom_call" | custom-call | bytes 1048576 | tf_op jit(solution)/shard_map/pallas_call | solution.py:96
  (5 shorter events, 0.1 us)
Async XLA Ops:
  0.0 3.0 %copy-start.4 = (s32[8]{0:T(128)S(1)}, s32[8]{0:T(128)}, u32[]{:S(2)}) copy-start(s32[8]{0:T(128)} %order_ref.1) | copy-start | bytes 100
  0.0 3.0 %collective-permute-start = (f32[128,1024]{1,0:T(8,128)}, f32[128,1024]{1,0:T(8,128)S(1)}, u32[]{:S(2)}, u32[]{:S(2)}) collective-permute-start(f32[128,1024]{1,0:T(8,128)} %bitcast.2), channel_id=1, source_target_pairs={{0,1},{1,0},{2,3},{3,2},{4,5},{5,4},{6,7},{7,6},{8,9},{9,8},{10,11... | collective-permute-start | bytes 1572872 | tf_op jit(solution)/shard_map/ppermute | solution.py:80
  0.5 15.3 %collective-permute-start.4 = (f32[128,1024]{1,0:T(8,128)}, f32[128,1024]{1,0:T(8,128)S(1)}, u32[]{:S(2)}, u32[]{:S(2)}) collective-permute-start(f32[128,1024]{1,0:T(8,128)} %bitcast.3), channel_id=1, source_target_pairs={{0,2},{1,3},{2,0},{3,1},{4,6},{5,7},{6,4},{7,5},{8,10},{9,11},{10,... | collective-permute-start | bytes 1572872 | tf_op jit(solution)/shard_map/ppermute | solution.py:80
  3.0 1.1 %copy-start = (f32[1,128,1024]{2,1,0:T(8,128)S(1)}, f32[1,128,1024]{2,1,0:T(8,128)}, u32[]{:S(2)}) copy-start(f32[1,128,1024]{2,1,0:T(8,128)} %param.5) | copy-start | bytes 1572868
  4.1 0.7 %copy-start.2 = (s32[8,4,8]{2,1,0:T(4,128)S(1)}, s32[8,4,8]{2,1,0:T(4,128)}, u32[]{:S(2)}) copy-start(s32[8,4,8]{2,1,0:T(4,128)} %pattern_ref.1) | copy-start | bytes 3076
  6.4 12.2 %collective-permute-start.1 = (f32[2,128,128]{2,1,0:T(8,128)S(1)}, f32[2,128,128]{2,1,0:T(8,128)S(1)}, u32[]{:S(2)}, u32[]{:S(2)}) collective-permute-start(f32[2,128,128]{2,1,0:T(8,128)S(1)} %get-tuple-element.9), channel_id=1, source_target_pairs={{0,4},{4,0},{8,12},{12,8},{16,20},{20,16},{24,28},{28,24},{1,5},{5... | collective-permute-start | bytes 393224 | tf_op jit(solution)/shard_map/ppermute | solution.py:80
  16.7 4.3 %collective-permute-start.5 = (f32[128,128]{1,0:T(8,128)S(1)}, f32[128,128]{1,0:T(8,128)S(1)}, u32[]{:S(2)}, u32[]{:S(2)}) collective-permute-start(f32[128,128]{1,0:T(8,128)S(1)} %shard_map.56), channel_id=1, source_target_pairs={{0,4},{4,0},{8,12},{12,8},{16,20},{20,16},{24,28},{28,24},{1,5},{5... | collective-permute-start | bytes 196616 | tf_op jit(solution)/shard_map/ppermute | solution.py:80
  18.6 9.7 %collective-permute-start.2 = (f32[2,128,128]{2,1,0:T(8,128)S(1)}, f32[2,128,128]{2,1,0:T(8,128)S(1)}, u32[]{:S(2)}, u32[]{:S(2)}) collective-permute-start(f32[2,128,128]{2,1,0:T(8,128)S(1)} %add.28), channel_id=1, source_target_pairs={{0,8},{4,12},{8,0},{12,4},{16,24},{20,28},{24,16},{28,20},{1,9},{5... | collective-permute-start | bytes 393224 | tf_op jit(solution)/shard_map/ppermute | solution.py:80
  21.1 4.3 %collective-permute-start.6 = (f32[128,128]{1,0:T(8,128)S(1)}, f32[128,128]{1,0:T(8,128)S(1)}, u32[]{:S(2)}, u32[]{:S(2)}) collective-permute-start(f32[128,128]{1,0:T(8,128)S(1)} %add.32), channel_id=1, source_target_pairs={{0,8},{4,12},{8,0},{12,4},{16,24},{20,28},{24,16},{28,20},{1,9},{5... | collective-permute-start | bytes 196616 | tf_op jit(solution)/shard_map/ppermute | solution.py:80
  25.4 8.0 %collective-permute-start.7 = (f32[128,128]{1,0:T(8,128)S(1)}, f32[128,128]{1,0:T(8,128)S(1)}, u32[]{:S(2)}, u32[]{:S(2)}) collective-permute-start(f32[128,128]{1,0:T(8,128)S(1)} %add.34), channel_id=1, source_target_pairs={{0,16},{4,20},{8,24},{12,28},{16,0},{20,4},{24,8},{28,12},{1,17},{... | collective-permute-start | bytes 196616 | tf_op jit(solution)/shard_map/ppermute | solution.py:80
  28.4 9.5 %copy-start.1 = (f32[128,512]{1,0:T(8,128)S(1)}, f32[128,512]{1,0:T(8,128)}, u32[]{:S(2)}) copy-start(f32[128,512]{1,0:T(8,128)} %panels_ref.1) | copy-start | bytes 786436
  28.4 9.4 %collective-permute-start.3 = (f32[2,128,128]{2,1,0:T(8,128)S(1)}, f32[2,128,128]{2,1,0:T(8,128)S(1)}, u32[]{:S(2)}, u32[]{:S(2)}) collective-permute-start(f32[2,128,128]{2,1,0:T(8,128)S(1)} %get-tuple-element.13), channel_id=1, source_target_pairs={{0,16},{4,20},{8,24},{12,28},{16,0},{20,4},{24,8},{28,12},{1,17},{... | collective-permute-start | bytes 393224 | tf_op jit(solution)/shard_map/ppermute | solution.py:80
  33.5 4.4 %copy-start.3 = (s32[2,2]{1,0:T(2,128)S(1)}, s32[2,2]{1,0:T(2,128)}, u32[]{:S(2)}) copy-start(s32[2,2]{1,0:T(2,128)} %targets_ref.1) | copy-start | bytes 52
  33.5 4.3 %collective-permute-start.8 = (f32[128,128]{1,0:T(8,128)S(1)}, f32[128,128]{1,0:T(8,128)S(1)}, u32[]{:S(2)}, u32[]{:S(2)}) collective-permute-start(f32[128,128]{1,0:T(8,128)S(1)} %select_add_fusion.1.own_ref), channel_id=1, source_target_pairs={{0,2},{1,3},{2,0},{3,1},{4,6},{5,7},{6,4},{7,5},{8,10},{9,11},{10,... | collective-permute-start | bytes 196616 | tf_op jit(solution)/shard_map/ppermute | solution.py:80
  35.3 2.5 %collective-permute-start.9 = (f32[128,128]{1,0:T(8,128)S(1)}, f32[128,128]{1,0:T(8,128)S(1)}, u32[]{:S(2)}, u32[]{:S(2)}) collective-permute-start(f32[128,128]{1,0:T(8,128)S(1)} %select_add_fusion.1.own_ref), channel_id=1, source_target_pairs={{0,1},{1,0},{2,3},{3,2},{4,5},{5,4},{6,7},{7,6},{8,9},{9,8},{10,11... | collective-permute-start | bytes 196616 | tf_op jit(solution)/shard_map/ppermute | solution.py:80
